TPU v7x, 32 devices: a whole 2x2x4 slice. The times are simulated.
32 devices in a mesh: rep: 2 (over y), gx: 16 (over z, x, core).
Axes of the slice: x: 2, y: 2, z: 4, core: 2. Of those that a mesh axis runs over, the one named last changes fastest.
Arguments:
- positions: float32 [3, 32768], P(None, ('rep', 'gx')), parts along dimension 1, may hold values from 0 to 8, as said below
- field: float32 [3, 32768], P(None, ('rep', 'gx')), parts along dimension 1, may hold values from -45 to 45
- inv_polar: float32 [32768], P(('rep', 'gx')), parts along dimension 0, may hold values from 2 to 8
- x_spline: float32 [2, 5, 32768], P(None, None, ('rep', 'gx')), parts along dimension 2, may hold values from -1 to 1, as said below
- yz_spline: float32 [4, 32768, 128], P(None, ('rep', 'gx')), parts along dimension 1, may hold values from -1 to 1, as said below
- tile_list: int32 [256, 7], P(('rep', 'gx')), parts along dimension 0, may hold values from 0 to 13, as said below
- tile_count: int32 [256], P(('rep', 'gx')), parts along dimension 0, may hold values from 1 to 7, as said below
Outputs:
- dipoles: float32 [3, 32768], P(None, ('rep', 'gx')), parts along dimension 1
- residual: float32 [3, 32768], P(None, ('rep', 'gx')), parts along dimension 1
There are 2 independent parts, one for each index of `rep`. A program takes and returns all parts, laid end to end along the dimension named above; each array names one. Nothing has to cross between parts.
Inputs may be any that keep to these rules, and one draw needn't show every extreme that they name: `positions`: the first coordinate of an atom of block b of its slab lies in [b, b + 1); the other two lie in [0, 2). x_spline[0, k, i] and x_spline[1, k, i] are the cardinal B-spline of order 5 and its derivative at u_i + 4 - k for some u_i in [0, 1). `yz_spline`: rows 0 and 1 hold, for each atom, the cardinal B-spline of order 5 and its derivative at u + 4 - k placed at grid line (t + k) mod 128 for k < 5, for some start t and some u in [0, 1), and zero elsewhere; rows 2 and 3 likewise with their own start and offset. `tile_list`: row g = s * 8 + b lists in rising order the extended blocks b + 3 + e, -3 <= e <= 3, for which global blocks g and g + e (modulo 128) are neighbours; being neighbours is symmetric and always holds for e = 0; entries from tile_count[g] on equal b + 3. `tile_count`: global block 0 has all 7 neighbours.
All inputs are finite; a program needn't handle non-finite values.
Results may differ from a plain program's by a relative error of at most 0.0003.
Values sent between devices are 32-bit elements; how exact they have to be, the bound alone decides.
A program may use at most 64 MiB of HBM per device.

v0:
```python
import jax
import jax.numpy as jnp
from jax import lax
from jax.experimental import pallas as pl
from jax.experimental.pallas import tpu as pltpu
from jax.sharding import PartitionSpec as P
import functools

GRID = 128
ORDER = 5
TILE = 128
HALO_BLK = 3
ITERS = 3


PAIR_C = 0.025
RECIP_C = 8192.0
DAMP = 0.0008
EXACT = lax.Precision.HIGHEST


def mode_of(freq, size):
    half_size = size // 2
    mode_num = jnp.where(freq <= half_size, freq, freq - half_size)
    weight = jnp.where((freq == 0) | (freq == half_size), 1.0 / size, 2.0 / size)
    return (mode_num.astype(jnp.float32), weight.astype(jnp.float32))


def basis_rows(size, points):
    freq = jnp.arange(size, dtype=jnp.int32)
    half_size = size // 2
    mode_num = jnp.where(freq <= half_size, freq, freq - half_size)
    phase = mode_num[:, None] * points[None, :] % size
    angle = phase.astype(jnp.float32) * (2.0 * jnp.pi / size)
    return jnp.where((freq <= half_size)[:, None], jnp.cos(angle), jnp.sin(angle))


def kernel_block(x_modes, x_weights, y_modes, y_weights, z_modes, z_weights):
    mode_sq = (
        x_modes[:, None, None] * x_modes[:, None, None]
        + y_modes[None, :, None] * y_modes[None, :, None]
        + z_modes[None, None, :] * z_modes[None, None, :]
    )
    safe_sq = jnp.where(mode_sq > 0, mode_sq, 1.0)
    green = jnp.where(mode_sq > 0, RECIP_C * jnp.exp(-DAMP * safe_sq) / safe_sq, 0.0)
    return green * x_weights[:, None, None] * y_weights[None, :, None] * z_weights[None, None, :]


F32 = jnp.float32
BF16 = jnp.bfloat16
VMEM = pl.BlockSpec(memory_space=pltpu.VMEM)


def split(x):
    high = x.astype(BF16)
    return high, (x - high.astype(F32)).astype(BF16)


def dot(a, b):
    return jnp.dot(a, b, preferred_element_type=F32)


def params(**more):
    return pltpu.CompilerParams(vmem_limit_bytes=56 * 1024 * 1024, **more)


def prep_kernel(yz_ref, rows_ref, yft_ref, zf_ref, zft_ref):
    rows = rows_ref[...]
    contract = (((1,), (1,)), ((), ()))
    for t in range(2):
        yft_ref[0, t] = lax.dot_general(
            rows, yz_ref[t], contract, precision=EXACT, preferred_element_type=F32
        )
    both = jnp.concatenate([yz_ref[2], yz_ref[3]], axis=0)
    high, low = split(
        lax.dot_general(both, rows, contract, precision=EXACT, preferred_element_type=F32)
    )
    zf_ref[0] = jnp.concatenate([high, low], axis=1)
    high, low = split(
        lax.dot_general(rows, both, contract, precision=EXACT, preferred_element_type=F32)
    )
    zft_ref[0] = jnp.concatenate([high, low], axis=0)


def prepare(yz_spline, rows, blocks):
    return pl.pallas_call(
        prep_kernel,
        grid=(blocks,),
        in_specs=[
            pl.BlockSpec((4, TILE, GRID), lambda b: (0, b, 0)),
            pl.BlockSpec((GRID, GRID), lambda b: (0, 0)),
        ],
        out_specs=[
            pl.BlockSpec((1, 2, GRID, TILE), lambda b: (b, 0, 0, 0)),
            pl.BlockSpec((1, 2 * TILE, 2 * GRID), lambda b: (b, 0, 0)),
            pl.BlockSpec((1, 2 * GRID, 2 * TILE), lambda b: (b, 0, 0)),
        ],
        out_shape=[
            jax.ShapeDtypeStruct((blocks, 2, GRID, TILE), F32),
            jax.ShapeDtypeStruct((blocks, 2 * TILE, 2 * GRID), BF16),
            jax.ShapeDtypeStruct((blocks, 2 * GRID, 2 * TILE), BF16),
        ],
        compiler_params=params(),
        name="prep",
    )(yz_spline, rows)


def spread_kernel(planes, ky_count, pv_ref, xs_ref, yft_ref, zf_ref, out_ref):
    blocks = pv_ref.shape[0]
    ranks = out_ref.shape[0]
    out_ref[...] = jnp.zeros_like(out_ref)

    def one_block(b, carry):
        base = b * planes // blocks
        y, dy = yft_ref[b, 0], yft_ref[b, 1]
        v0, v1, v2 = (pv_ref[b, 3 + c : 4 + c, :] for c in range(3))
        highs, lows = [], []
        for k in range(ORDER):
            x, dx = xs_ref[b, k : k + 1, :], xs_ref[b, ORDER + k : ORDER + k + 1, :]
            lead = (v0 * dx) * y + (v1 * x) * dy
            high, low = split(jnp.concatenate([lead, (v2 * x) * y], axis=1))
            highs.append(high)
            lows.append(low)
        weights = zf_ref[b]
        wide = dot(jnp.concatenate(highs, axis=0), weights)
        total = (
            wide[:, :GRID] + wide[:, GRID:] + dot(jnp.concatenate(lows, axis=0), weights[:, :GRID])
        )
        for k in range(ORDER):
            part = total[k * GRID : (k + 1) * GRID].reshape(ranks, ky_count, GRID)
            out_ref[:, base + k, :ky_count, :] += part
        return carry

    lax.fori_loop(0, blocks, one_block, 0)


def gather_kernel(planes, ky_count, ret_ref, xs_ref, yft_ref, zft_ref, out_ref, wide_ref, low_ref):
    blocks = xs_ref.shape[0]
    extent = ret_ref.shape[1]
    for p in range(extent):
        high, low = split(ret_ref[:, p, :ky_count, :].reshape(GRID, GRID))
        wide_ref[p] = jnp.concatenate([high, high], axis=1)
        low_ref[p] = low

    def one_block(b, carry):
        base = b * planes // blocks
        weights = zft_ref[b]
        wide = wide_ref[pl.ds(base, ORDER)].reshape(ORDER * GRID, 2 * GRID)
        low = low_ref[pl.ds(base, ORDER)].reshape(ORDER * GRID, GRID)
        sums = dot(wide, weights) + dot(low, weights[:GRID])
        one = two = three = 0.0
        for k in range(ORDER):
            x, dx = xs_ref[b, k : k + 1, :], xs_ref[b, ORDER + k : ORDER + k + 1, :]
            plain = sums[k * GRID : (k + 1) * GRID, :TILE]
            one += dx * plain
            two += x * plain
            three += x * sums[k * GRID : (k + 1) * GRID, TILE:]
        y, dy = yft_ref[b, 0], yft_ref[b, 1]
        out_ref[b, 0:1] = jnp.sum(y * one, axis=0, keepdims=True)
        out_ref[b, 1:2] = jnp.sum(dy * two, axis=0, keepdims=True)
        out_ref[b, 2:3] = jnp.sum(y * three, axis=0, keepdims=True)
        return carry

    lax.fori_loop(0, blocks, one_block, 0)


def pair_kernel(near_ref, pv_ref, before_ref, after_ref, out_ref, ext_ref, col_ref, acc_ref):
    blocks = pv_ref.shape[0]
    ext_blocks = ext_ref.shape[0]
    reach = 2 * HALO_BLK + 1
    first_row = lax.broadcasted_iota(jnp.int32, (HALO_BLK, 8, TILE), 1) == 0
    ext_ref[:HALO_BLK] = before_ref[...] + jnp.where(first_row, -1.0 * blocks, 0.0)
    ext_ref[HALO_BLK : HALO_BLK + blocks] = pv_ref[...]
    ext_ref[HALO_BLK + blocks :] = after_ref[...] + jnp.where(first_row, 1.0 * blocks, 0.0)
    acc_ref[...] = jnp.zeros_like(acc_ref)
    lag = lax.broadcasted_iota(jnp.int32, (8, TILE), 1) - lax.broadcasted_iota(
        jnp.int32, (8, TILE), 0
    )

    def one_source(e, carry):
        for c in range(6):
            col_ref[c] = jnp.broadcast_to(ext_ref[e, c : c + 1, :], (TILE, TILE)).T

        def one_home(b, inner):
            @pl.when(near_ref[b * reach + e - b] > 0)
            def _():
                home = [jnp.broadcast_to(pv_ref[b, c : c + 1, :], (8, TILE)) for c in range(3)]
                shift = jnp.where(e == b + HALO_BLK, 0, 4 * TILE)
                direct = [jnp.zeros((8, TILE), F32) for c in range(3)]
                tilted = [jnp.zeros((8, TILE), F32) for c in range(3)]
                for j in range(TILE // 8):
                    rows = slice(8 * j, 8 * j + 8)
                    r = [home[c] - col_ref[c, rows, :] for c in range(3)]
                    v = [col_ref[3 + c, rows, :] for c in range(3)]
                    inverse = lax.rsqrt(r[0] * r[0] + r[1] * r[1] + r[2] * r[2] + 1.0)
                    inverse = jnp.where(lag != 8 * j + shift, inverse, 0.0)
                    square = inverse * inverse
                    third = square * inverse
                    weight = third * square * (r[0] * v[0] + r[1] * v[1] + r[2] * v[2])
                    for c in range(3):
                        direct[c] += third * v[c]
                        tilted[c] += weight * r[c]
                for c in range(3):
                    acc_ref[b, c] += direct[c] - 3.0 * tilted[c]

            return inner

        lo = jnp.maximum(e - (reach - 1), 0)
        hi = jnp.minimum(e + 1, blocks)
        lax.fori_loop(lo, hi, one_home, 0)
        return carry

    lax.fori_loop(0, ext_blocks, one_source, 0)
    for b in range(blocks):
        for c in range(3):
            out_ref[b, c : c + 1] = PAIR_C * jnp.sum(acc_ref[b, c], axis=0, keepdims=True)


def greet(ranks, me):
    barrier = pltpu.get_barrier_semaphore()

    def signal(d, carry):
        pl.semaphore_signal(
            barrier,
            inc=1,
            device_id={"gx": lax.rem(me + d, ranks)},
            device_id_type=pl.DeviceIdType.MESH,
        )
        return carry

    lax.fori_loop(1, ranks, signal, 0)
    pl.semaphore_wait(barrier, ranks - 1)


def exchange(ranks, me, source, target, local_sem, send_sem, recv_sem):
    def copy(d, slot):
        peer = lax.rem(me + d, ranks)
        return pltpu.make_async_remote_copy(
            src_ref=source(peer),
            dst_ref=target(slot),
            send_sem=send_sem.at[d],
            recv_sem=recv_sem.at[d],
            device_id={"gx": peer},
            device_id_type=pl.DeviceIdType.MESH,
        )

    def start(d, carry):
        copy(d, me).start()
        return carry

    def finish(d, carry):
        copy(d, lax.rem(me - d + ranks, ranks)).wait()
        return carry

    lax.fori_loop(1, ranks, start, 0)
    own = pltpu.make_async_copy(source(me), target(me), local_sem)
    own.start()

    def wait():
        own.wait()
        lax.fori_loop(1, ranks, finish, 0)

    return wait


def middle_kernel(
    ranks, ky_count, spec_ref, pv_ref, green_ref, across_ref, back_ref,
    ret_ref, before_ref, after_ref,
    recv_ref, done_ref, local_sems, send1, recv1, send2, recv2, halo_send, halo_recv,
):
    me = lax.axis_index("gx")
    blocks = pv_ref.shape[0]
    extent = spec_ref.shape[1]
    rows = ranks * extent
    greet(ranks, me)
    halos = []
    for t, (piece, into, step) in enumerate(
        (
            (pv_ref.at[pl.ds(blocks - HALO_BLK, HALO_BLK)], before_ref, 1),
            (pv_ref.at[pl.ds(0, HALO_BLK)], after_ref, ranks - 1),
        )
    ):
        halos.append(
            pltpu.make_async_remote_copy(
                src_ref=piece,
                dst_ref=into,
                send_sem=halo_send.at[t],
                recv_sem=halo_recv.at[t],
                device_id={"gx": lax.rem(me + step, ranks)},
                device_id_type=pl.DeviceIdType.MESH,
            )
        )
        halos[-1].start()
    wait = exchange(
        ranks, me, lambda d: spec_ref.at[d], lambda d: recv_ref.at[d], local_sems.at[0], send1, recv1
    )
    across_high, across_low = split(across_ref[...])
    back_high, back_low = split(back_ref[...])
    wait()
    lines_in = recv_ref.reshape(rows * 8, GRID)
    lines_out = done_ref.reshape(rows * 8, GRID)
    for q in range(ky_count):
        high, low = split(lines_in[pl.ds(q, rows, stride=8), :])
        wide = dot(across_high, jnp.concatenate([high, low], axis=1))
        line = wide[:, :GRID] + wide[:, GRID:] + dot(across_low, high)
        high, low = split(line * green_ref[q])
        wide = dot(back_high, jnp.concatenate([high, low], axis=1))
        lines_out[pl.ds(q, rows, stride=8), :] = (
            wide[:, :GRID] + wide[:, GRID:] + dot(back_low, high)
        )
    wait = exchange(
        ranks, me, lambda d: done_ref.at[d], lambda d: ret_ref.at[d], local_sems.at[1], send2, recv2
    )
    for halo in halos:
        halo.wait()
    wait()


def middle(spec, pv, green, across, back, ranks, ky_count):
    dma = pltpu.SemaphoreType.DMA
    halo = jax.ShapeDtypeStruct((HALO_BLK, 8, TILE), F32)
    return pl.pallas_call(
        functools.partial(middle_kernel, ranks, ky_count),
        in_specs=[VMEM] * 5,
        out_specs=[VMEM] * 3,
        out_shape=[jax.ShapeDtypeStruct(spec.shape, F32), halo, halo],
        scratch_shapes=[
            pltpu.VMEM(spec.shape, F32),
            pltpu.VMEM(spec.shape, F32),
            dma((2,)), dma((ranks,)), dma((ranks,)), dma((ranks,)), dma((ranks,)),
            dma((2,)), dma((2,)),
        ],
        compiler_params=params(collective_id=0, has_side_effects=True),
        name="middle",
    )(spec, pv, green, across, back)


def total_kernel(ranks, x_ref, out_ref, slots, local_sem, send_sem, recv_sem):
    me = lax.axis_index("gx")
    greet(ranks, me)
    wait = exchange(
        ranks, me, lambda d: x_ref, lambda d: slots.at[d], local_sem.at[0], send_sem, recv_sem
    )
    wait()
    out_ref[...] = jnp.sum(slots[...], axis=0)


def total(x, ranks):
    dma = pltpu.SemaphoreType.DMA
    return pl.pallas_call(
        functools.partial(total_kernel, ranks),
        in_specs=[VMEM],
        out_specs=VMEM,
        out_shape=jax.ShapeDtypeStruct(x.shape, F32),
        scratch_shapes=[
            pltpu.VMEM((ranks,) + x.shape, F32), dma((1,)), dma((ranks,)), dma((ranks,)),
        ],
        compiler_params=params(collective_id=1, has_side_effects=True),
        name="total",
    )(x)


def per_device(positions, field, inv_polar, x_spline, yz_spline, tile_list, tile_count):
    ranks = lax.axis_size("gx")
    rank_index = lax.axis_index("gx")
    atoms_here = positions.shape[1]
    planes = GRID // ranks
    extent = planes + 4
    blocks = atoms_here // TILE
    reach = 2 * HALO_BLK + 1
    ky_count = GRID // ranks

    def blocked(x):
        return x.reshape(-1, blocks, TILE).transpose(1, 0, 2)

    all_freq = jnp.arange(GRID, dtype=jnp.int32)
    fourier_rows = basis_rows(GRID, all_freq)
    ky_freq = rank_index * ky_count + jnp.arange(ky_count, dtype=jnp.int32)
    full_modes, full_weights = mode_of(all_freq, GRID)
    ky_modes, ky_weights = mode_of(ky_freq, GRID)
    green = kernel_block(ky_modes, ky_weights, full_modes, full_weights, full_modes, full_weights)
    source_rows = jnp.arange(ranks * extent, dtype=jnp.int32)
    points = (source_rows // extent * planes - 2 + source_rows % extent) % GRID
    across = basis_rows(GRID, points)
    back = across.T
    slots = jnp.arange(tile_list.shape[1], dtype=jnp.int32)
    wanted = jnp.arange(blocks, dtype=jnp.int32)[:, None] + jnp.arange(reach, dtype=jnp.int32)
    live = (slots[None, :] < tile_count[:, None])[:, :, None]
    near = jnp.any((tile_list[:, :, None] == wanted[:, None, :]) & live, axis=1)
    near = near.astype(jnp.int32).reshape(-1)
    yft, zf, zft = prepare(yz_spline, fourier_rows, blocks)
    xs = blocked(x_spline.reshape(2 * ORDER, atoms_here))
    pos = blocked(positions)
    polar = inv_polar.reshape(blocks, 1, TILE)
    spec_shape = jax.ShapeDtypeStruct((ranks, extent, 8, GRID), F32)
    rows_shape = jax.ShapeDtypeStruct((blocks, 3, TILE), F32)

    def apply(vector):
        pv = jnp.concatenate([pos, vector, jnp.zeros((blocks, 2, TILE), F32)], axis=1)
        spec = pl.pallas_call(
            functools.partial(spread_kernel, planes, ky_count),
            in_specs=[VMEM] * 4,
            out_specs=VMEM,
            out_shape=spec_shape,
            compiler_params=params(),
            name="spread",
        )(pv, xs, yft, zf)
        ret, before, after = middle(spec, pv, green, across, back, ranks, ky_count)
        pair = pl.pallas_call(
            pair_kernel,
            in_specs=[pl.BlockSpec(memory_space=pltpu.SMEM)] + [VMEM] * 3,
            out_specs=VMEM,
            out_shape=rows_shape,
            scratch_shapes=[
                pltpu.VMEM((blocks + 2 * HALO_BLK, 8, TILE), F32),
                pltpu.VMEM((6, TILE, TILE), F32),
                pltpu.VMEM((blocks, 3, 8, TILE), F32),
            ],
            compiler_params=params(),
            name="pair",
        )(near, pv, before, after)
        far = pl.pallas_call(
            functools.partial(gather_kernel, planes, ky_count),
            in_specs=[VMEM] * 4,
            out_specs=VMEM,
            out_shape=rows_shape,
            scratch_shapes=[
                pltpu.VMEM((extent, GRID, 2 * GRID), BF16),
                pltpu.VMEM((extent, GRID, GRID), BF16),
            ],
            compiler_params=params(),
            name="gather",
        )(ret, xs, yft, zft)
        return polar * vector + far - pair

    def paired(residual, precond, applied):
        first = jnp.sum(residual * precond, axis=(0, 1))
        second = jnp.sum(applied * precond, axis=(0, 1))
        sums = total(jnp.stack([first, second] + [jnp.zeros_like(first)] * 6), ranks)
        sums = jnp.sum(sums, axis=1)
        return sums[0], sums[1]

    residual = blocked(field)
    dipoles = jnp.zeros_like(residual)
    precond = residual / polar
    applied = apply(precond)
    rz_now, curvature = paired(residual, precond, applied)
    step_size = rz_now / curvature
    direction = precond
    applied_dir = applied
    for sweep_index in range(ITERS):
        dipoles = dipoles + step_size * direction
        residual = residual - step_size * applied_dir
        if sweep_index + 1 < ITERS:
            precond = residual / polar
            applied = apply(precond)
            rz_next, curvature = paired(residual, precond, applied)
            beta_ratio = rz_next / rz_now
            step_size = rz_next / (curvature - beta_ratio * rz_next / step_size)
            direction = precond + beta_ratio * direction
            applied_dir = applied + beta_ratio * applied_dir
            rz_now = rz_next

    def flat(x):
        return x.transpose(1, 0, 2).reshape(3, atoms_here)

    return flat(dipoles), flat(residual)


def solution(mesh):
    placed = (
        P(None, ("rep", "gx")),
        P(None, ("rep", "gx")),
        P(("rep", "gx")),
        P(None, None, ("rep", "gx")),
        P(None, ("rep", "gx"), None),
        P(("rep", "gx"), None),
        P(("rep", "gx")),
    )
    return jax.shard_map(
        per_device,
        mesh=mesh,
        in_specs=placed,
        out_specs=(P(None, ("rep", "gx")), P(None, ("rep", "gx"))),
        check_vma=False,
    )
```

profile of v0, /device:TPU:0, one launch (start us, length us, event | category | flops | bytes accessed | tf_op | source)
XLA Modules:
  0.0 253.9 jit_solution(12783782483471426680)
XLA Ops:
  3.8 1.4 fusion.20.pv_ref
  5.3 1.0 sine_select_fusion.2.rows_ref
  7.7 1.1 sine_select_fusion.1.back_ref
  8.8 1.2 sine_select_fusion.across_ref
  10.0 1.1 fusion.5.green_ref
  11.1 8.2 %prep.1 = (f32[8,2,128,128]{3,2,1,0:T(8,128)}, bf16[8,256,256]{2,1,0:T(8,128)(2,1)}, bf16[8,256,256]{2,1,0:T(8,128)(2,1)}) custom-call(f32[4,1024,128]{2,1,0:T(8,128)} %yz_ref.1, f32[128,128]{1,0:T(8,128)} %sine_select_fusion.2.rows_ref), custom_call_target="tpu_custom_call" | custom-call | tf_op jit(solution)/shard_map/prep/pallas_call | solution.py:86
  19.3 5.3 %spread.3.spec_ref = f32[16,12,8,128]{3,2,1,0:T(8,128)} custom-call(f32[8,8,128]{2,1,0:T(8,128)} %fusion.20.pv_ref, f32[8,10,128]{2,1,0:T(8,128)} %bitcast.45, f32[8,2,128,128]{3,2,1,0:T(8,128)} %get-tuple-element.14.yft_ref, bf16[8,256,256]{2,1,0:T(8,128)(2,1)} %get-tuple-element.15.zf_ref), custom_call_target="tpu_custom_call" | custom-call | tf_op jit(solution)/shard_map/spread/pallas_call | solution.py:400
  24.6 40.1 %middle.3 = (f32[16,12,8,128]{3,2,1,0:T(8,128)}, f32[3,8,128]{2,1,0:T(8,128)}, f32[3,8,128]{2,1,0:T(8,128)}) custom-call(f32[16,12,8,128]{3,2,1,0:T(8,128)} %spread.3.spec_ref, f32[8,8,128]{2,1,0:T(8,128)} %fusion.20.pv_ref, f32[8,128,128]{2,1,0:T(8,128)} %fusion.5.green_ref, f32[128,192]{1,0:T(8,128)} %sine_select_fusion.across_ref, ...), custom_call_target="tpu_custom_call" | custom-call | tf_op jit(solution)/shard_map/middle/pallas_call | solution.py:322
  64.8 7.6 %pair.3 = f32[8,3,128]{2,1,0:T(4,128)} custom-call(s32[56]{0:T(128)} %reshape.187.near_ref, f32[8,8,128]{2,1,0:T(8,128)} %fusion.20.pv_ref, f32[3,8,128]{2,1,0:T(8,128)} %get-tuple-element.18.before_ref, f32[3,8,128]{2,1,0:T(8,128)} %get-tuple-element.19.after_ref), custom_call_target="tpu_custom_call" | custom-call | tf_op jit(solution)/shard_map/pair/pallas_call | solution.py:409
  72.4 5.4 %gather.3 = f32[8,3,128]{2,1,0:T(4,128)} custom-call(f32[16,12,8,128]{3,2,1,0:T(8,128)} %get-tuple-element.16.ret_ref, f32[8,10,128]{2,1,0:T(8,128)} %bitcast.46, f32[8,2,128,128]{3,2,1,0:T(8,128)} %get-tuple-element.14.yft_ref, bf16[8,256,256]{2,1,0:T(8,128)(2,1)} %get-tuple-element.17.zft_ref), custom_call_target="tpu_custom_call" | custom-call | tf_op jit(solution)/shard_map/gather/pallas_call | solution.py:422
  79.2 13.7 %total.3 = f32[8,128]{1,0:T(8,128)} custom-call(f32[8,128]{1,0:T(8,128)} %maximum_maximum_fusion.x_ref), custom_call_target="tpu_custom_call" | custom-call | tf_op jit(solution)/shard_map/total/pallas_call | solution.py:350
  92.9 0.8 reduce_sum.83
  96.4 5.3 %spread.4.spec_ref = f32[16,12,8,128]{3,2,1,0:T(8,128)} custom-call(f32[8,8,128]{2,1,0:T(8,128)} %fusion.21.pv_ref, f32[8,10,128]{2,1,0:T(8,128)} %bitcast.47, f32[8,2,128,128]{3,2,1,0:T(8,128)} %get-tuple-element.14.yft_ref, bf16[8,256,256]{2,1,0:T(8,128)(2,1)} %get-tuple-element.15.zf_ref), custom_call_target="tpu_custom_call" | custom-call | tf_op jit(solution)/shard_map/spread/pallas_call | solution.py:400
  101.7 38.2 %middle.4 = (f32[16,12,8,128]{3,2,1,0:T(8,128)}, f32[3,8,128]{2,1,0:T(8,128)}, f32[3,8,128]{2,1,0:T(8,128)}) custom-call(f32[16,12,8,128]{3,2,1,0:T(8,128)} %spread.4.spec_ref, f32[8,8,128]{2,1,0:T(8,128)} %fusion.21.pv_ref, f32[8,128,128]{2,1,0:T(8,128)} %fusion.5.green_ref, f32[128,192]{1,0:T(8,128)} %sine_select_fusion.across_ref, ...), custom_call_target="tpu_custom_call" | custom-call | tf_op jit(solution)/shard_map/middle/pallas_call | solution.py:322
  139.9 7.6 %pair.4 = f32[8,3,128]{2,1,0:T(4,128)} custom-call(s32[56]{0:T(128)} %reshape.187.near_ref, f32[8,8,128]{2,1,0:T(8,128)} %fusion.21.pv_ref, f32[3,8,128]{2,1,0:T(8,128)} %get-tuple-element.21.before_ref, f32[3,8,128]{2,1,0:T(8,128)} %get-tuple-element.22.after_ref), custom_call_target="tpu_custom_call" | custom-call | tf_op jit(solution)/shard_map/pair/pallas_call | solution.py:409
  147.6 5.4 %gather.4 = f32[8,3,128]{2,1,0:T(4,128)} custom-call(f32[16,12,8,128]{3,2,1,0:T(8,128)} %get-tuple-element.20.ret_ref, f32[8,10,128]{2,1,0:T(8,128)} %bitcast.48, f32[8,2,128,128]{3,2,1,0:T(8,128)} %get-tuple-element.14.yft_ref, bf16[8,256,256]{2,1,0:T(8,128)(2,1)} %get-tuple-element.17.zft_ref), custom_call_target="tpu_custom_call" | custom-call | tf_op jit(solution)/shard_map/gather/pallas_call | solution.py:422
  154.3 14.0 %total.4 = f32[8,128]{1,0:T(8,128)} custom-call(f32[8,128]{1,0:T(8,128)} %maximum_maximum_fusion.1.x_ref), custom_call_target="tpu_custom_call" | custom-call | tf_op jit(solution)/shard_map/total/pallas_call | solution.py:350
  168.3 0.8 reduce_sum.86
  175.1 5.3 %spread.5.spec_ref = f32[16,12,8,128]{3,2,1,0:T(8,128)} custom-call(f32[8,8,128]{2,1,0:T(8,128)} %fusion.22.pv_ref, f32[8,10,128]{2,1,0:T(8,128)} %bitcast.49, f32[8,2,128,128]{3,2,1,0:T(8,128)} %get-tuple-element.14.yft_ref, bf16[8,256,256]{2,1,0:T(8,128)(2,1)} %get-tuple-element.15.zf_ref), custom_call_target="tpu_custom_call" | custom-call | tf_op jit(solution)/shard_map/spread/pallas_call | solution.py:400
  180.4 38.3 %middle.5 = (f32[16,12,8,128]{3,2,1,0:T(8,128)}, f32[3,8,128]{2,1,0:T(8,128)}, f32[3,8,128]{2,1,0:T(8,128)}) custom-call(f32[16,12,8,128]{3,2,1,0:T(8,128)} %spread.5.spec_ref, f32[8,8,128]{2,1,0:T(8,128)} %fusion.22.pv_ref, f32[8,128,128]{2,1,0:T(8,128)} %fusion.5.green_ref, f32[128,192]{1,0:T(8,128)} %sine_select_fusion.across_ref, ...), custom_call_target="tpu_custom_call" | custom-call | tf_op jit(solution)/shard_map/middle/pallas_call | solution.py:322
  218.7 7.6 %pair.5 = f32[8,3,128]{2,1,0:T(4,128)} custom-call(s32[56]{0:T(128)} %reshape.187.near_ref, f32[8,8,128]{2,1,0:T(8,128)} %fusion.22.pv_ref, f32[3,8,128]{2,1,0:T(8,128)} %get-tuple-element.24.before_ref, f32[3,8,128]{2,1,0:T(8,128)} %get-tuple-element.25.after_ref), custom_call_target="tpu_custom_call" | custom-call | tf_op jit(solution)/shard_map/pair/pallas_call | solution.py:409
  226.4 5.4 %gather.5 = f32[8,3,128]{2,1,0:T(4,128)} custom-call(f32[16,12,8,128]{3,2,1,0:T(8,128)} %get-tuple-element.23.ret_ref, f32[8,10,128]{2,1,0:T(8,128)} %bitcast.50, f32[8,2,128,128]{3,2,1,0:T(8,128)} %get-tuple-element.14.yft_ref, bf16[8,256,256]{2,1,0:T(8,128)(2,1)} %get-tuple-element.17.zft_ref), custom_call_target="tpu_custom_call" | custom-call | tf_op jit(solution)/shard_map/gather/pallas_call | solution.py:422
  233.1 13.9 %total.5 = f32[8,128]{1,0:T(8,128)} custom-call(f32[8,128]{1,0:T(8,128)} %maximum_maximum_fusion.2.x_ref), custom_call_target="tpu_custom_call" | custom-call | tf_op jit(solution)/shard_map/total/pallas_call | solution.py:350
  252.5 1.4 subtract_bitcast_fusion
  (46 shorter events, 12.9 us)
Async XLA Ops:
  24.6 53.1 %copy-start = (f32[3,1024]{1,0:T(4,128)S(1)}, f32[3,1024]{1,0:T(4,128)}, u32[]{:S(2)}) copy-start(f32[3,1024]{1,0:T(4,128)} %param.8) | copy-start | bytes 36868
  24.6 53.1 %copy-start.1 = (f32[1024]{0:T(1024)S(1)}, f32[1024]{0:T(1024)}, u32[]{:S(2)}) copy-start(f32[1024]{0:T(1024)} %param.9) | copy-start | bytes 12292
  24.6 71.0 %copy-start.3 = (f32[3,1024]{1,0:T(4,128)S(1)}, f32[3,1024]{1,0:T(4,128)}, u32[]{:S(2)}) copy-start(f32[3,1024]{1,0:T(4,128)} %param.7) | copy-start | bytes 36868
  72.4 5.4 %copy-start.4 = (f32[8,3,128]{2,1,0:T(4,128)S(1)}, f32[8,3,128]{2,1,0:T(4,128)}, u32[]{:S(2)}) copy-start(f32[8,3,128]{2,1,0:T(4,128)} %pair.3) | copy-start | bytes 36868
  147.6 5.4 %copy-start.5 = (f32[8,3,128]{2,1,0:T(4,128)S(1)}, f32[8,3,128]{2,1,0:T(4,128)}, u32[]{:S(2)}) copy-start(f32[8,3,128]{2,1,0:T(4,128)} %pair.4) | copy-start | bytes 36868
  226.4 5.4 %copy-start.2 = (f32[8,3,128]{2,1,0:T(4,128)S(1)}, f32[8,3,128]{2,1,0:T(4,128)}, u32[]{:S(2)}) copy-start(f32[8,3,128]{2,1,0:T(4,128)} %pair.5) | copy-start | bytes 36868
where the time goes:
time: 256 us; the launch traced here: 254 us
  Pallas kernels  221 us (86%)
  other arithmetic  16.8 us (7%)
  between operations  10.9 us (4%)
  local copies, waits for them, and re-layouts  4.81 us (2%)
    pallas_call x3, Pallas kernels, middle(): pl.pallas_call(functools.partial(middle_kernel, ranks, ky_count), in_spec...  117 us
    pallas_call x3, Pallas kernels, total(): pl.pallas_call(functools.partial(total_kernel, ranks), in_specs=[VMEM], o...  41.6 us
    pallas_call x3, Pallas kernels, apply(): pl.pallas_call(pair_kernel, in_specs=[pl.BlockSpec(memory_space=pltpu.SME...  22.9 us
    pallas_call x3, Pallas kernels, apply(): pl.pallas_call(functools.partial(gather_kernel, planes, ky_count), in_spe...  16.1 us
    pallas_call x3, Pallas kernels, apply(): pl.pallas_call(functools.partial(spread_kernel, planes, ky_count), in_spe...  15.9 us
    pallas_call x1, Pallas kernels, prepare(): pl.pallas_call(prep_kernel, grid=(blocks,), in_specs=[pl.BlockSpec((4, TI...  8.21 us

commit v1 on v0

--- a/solution.py
+++ b/solution.py
@@ -5,6 +5,7 @@
 from jax.experimental.pallas import tpu as pltpu
 from jax.sharding import PartitionSpec as P
 import functools
+import numpy as np
 
 GRID = 128
 ORDER = 5
@@ -65,21 +66,21 @@
 
 
 def prep_kernel(yz_ref, rows_ref, yft_ref, zf_ref, zft_ref):
-    rows = rows_ref[...]
-    contract = (((1,), (1,)), ((), ()))
-    for t in range(2):
-        yft_ref[0, t] = lax.dot_general(
-            rows, yz_ref[t], contract, precision=EXACT, preferred_element_type=F32
-        )
-    both = jnp.concatenate([yz_ref[2], yz_ref[3]], axis=0)
-    high, low = split(
-        lax.dot_general(both, rows, contract, precision=EXACT, preferred_element_type=F32)
-    )
-    zf_ref[0] = jnp.concatenate([high, low], axis=1)
-    high, low = split(
-        lax.dot_general(rows, both, contract, precision=EXACT, preferred_element_type=F32)
-    )
-    zft_ref[0] = jnp.concatenate([high, low], axis=0)
+    rows = jnp.concatenate(split(rows_ref[...]), axis=0)
+
+    def transformed(t):
+        high, low = split(jnp.concatenate([yz_ref[t], yz_ref[t + 1]], axis=0))
+        contract = (((1,), (1,)), ((), ()))
+        wide = lax.dot_general(rows, high, contract, preferred_element_type=F32)
+        more = lax.dot_general(rows[:GRID], low, contract, preferred_element_type=F32)
+        return wide[:GRID] + wide[GRID:] + more
+
+    lines = transformed(0)
+    yft_ref[0, 0] = lines[:, :TILE]
+    yft_ref[0, 1] = lines[:, TILE:]
+    lines = transformed(2)
+    zft_ref[0] = jnp.concatenate(split(lines), axis=0)
+    zf_ref[0] = jnp.concatenate(split(lines.T), axis=1)
 
 
 def prepare(yz_spline, rows, blocks):
@@ -134,7 +135,10 @@
     lax.fori_loop(0, blocks, one_block, 0)
 
 
-def gather_kernel(planes, ky_count, ret_ref, xs_ref, yft_ref, zft_ref, out_ref, wide_ref, low_ref):
+def gather_kernel(
+    planes, ky_count, ret_ref, xs_ref, yft_ref, zft_ref, pair_ref, pv_ref, polar_ref,
+    next_ref, pv_next_ref, wide_ref, low_ref,
+):
     blocks = xs_ref.shape[0]
     extent = ret_ref.shape[1]
     for p in range(extent):
@@ -156,9 +160,14 @@
             two += x * plain
             three += x * sums[k * GRID : (k + 1) * GRID, TILE:]
         y, dy = yft_ref[b, 0], yft_ref[b, 1]
-        out_ref[b, 0:1] = jnp.sum(y * one, axis=0, keepdims=True)
-        out_ref[b, 1:2] = jnp.sum(dy * two, axis=0, keepdims=True)
-        out_ref[b, 2:3] = jnp.sum(y * three, axis=0, keepdims=True)
+        far = jnp.concatenate(
+            [jnp.sum(t, axis=0, keepdims=True) for t in (y * one, dy * two, y * three)], axis=0
+        )
+        following = pair_ref[b] - far
+        next_ref[b] = following
+        pv_next_ref[b, 0:3] = pv_ref[b, 0:3]
+        pv_next_ref[b, 3:6] = following / polar_ref[b]
+        pv_next_ref[b, 6:8] = jnp.zeros((2, TILE), F32)
         return carry
 
     lax.fori_loop(0, blocks, one_block, 0)
@@ -335,29 +344,91 @@
     )(spec, pv, green, across, back)
 
 
-def total_kernel(ranks, x_ref, out_ref, slots, local_sem, send_sem, recv_sem):
+def combine(weights, parts):
+    terms = [w * p for w, p in zip(weights, parts) if w is not None]
+    return functools.reduce(jnp.add, terms)
+
+
+def scaled(a, x, y):
+    pairs = zip(x, y)
+    return [p if q is None else (a * q if p is None else p + a * q) for p, q in pairs]
+
+
+def solve_kernel(
+    ranks, b0_ref, b1_ref, b2_ref, b3_ref, polar_ref,
+    dipoles_ref, residual_ref, part_ref, slots, local_sem, send_sem, recv_sem,
+):
     me = lax.axis_index("gx")
+    bases = [ref[...] for ref in (b0_ref, b1_ref, b2_ref, b3_ref)]
+    soft = [b / polar_ref[...] for b in bases]
+    count = ITERS + 1
+    place = {}
+    part_ref[...] = jnp.zeros_like(part_ref)
+    for i in range(count):
+        for j in range(i, count):
+            place[i, j] = place[j, i] = row = len(set(place.values()))
+            part_ref[row : row + 1] = jnp.sum(
+                jnp.sum(bases[i] * soft[j], axis=0), axis=0, keepdims=True
+            )
     greet(ranks, me)
     wait = exchange(
-        ranks, me, lambda d: x_ref, lambda d: slots.at[d], local_sem.at[0], send_sem, recv_sem
+        ranks, me, lambda d: part_ref, lambda d: slots.at[d], local_sem.at[0], send_sem, recv_sem
     )
     wait()
-    out_ref[...] = jnp.sum(slots[...], axis=0)
-
-
-def total(x, ranks):
+    sums = jnp.sum(jnp.sum(slots[...], axis=0), axis=1, keepdims=True)
+    sums = jnp.broadcast_to(sums, (sums.shape[0], TILE))
+
+    def inner(x, y):
+        value = None
+        for i in range(count):
+            for j in range(count):
+                if x[i] is not None and y[j] is not None:
+                    row = place[i, j]
+                    term = x[i] * y[j] * sums[row : row + 1]
+                    value = term if value is None else value + term
+        return value
+
+    none = [None] * (count - 1)
+    residual = [jnp.ones((1, TILE), F32)] + none
+    direction = list(residual)
+    dipoles = [None] * count
+    rz_now = inner(residual, residual)
+    for sweep in range(ITERS):
+        image = scaled(-1.0, direction, [None] + direction[:-1])
+        step = rz_now / inner(direction, image)
+        dipoles = scaled(step, dipoles, direction)
+        residual = scaled(-step, residual, image)
+        if sweep + 1 < ITERS:
+            rz_next = inner(residual, residual)
+            direction = scaled(rz_next / rz_now, residual, direction)
+            rz_now = rz_next
+    dipoles_ref[...] = combine(dipoles, soft)
+    residual_ref[...] = combine(residual, bases)
+
+
+def solve(bases, polar, ranks):
     dma = pltpu.SemaphoreType.DMA
+    shape = bases[0].shape
     return pl.pallas_call(
-        functools.partial(total_kernel, ranks),
-        in_specs=[VMEM],
-        out_specs=VMEM,
-        out_shape=jax.ShapeDtypeStruct(x.shape, F32),
+        functools.partial(solve_kernel, ranks),
+        in_specs=[VMEM] * 5,
+        out_specs=[VMEM] * 2,
+        out_shape=[jax.ShapeDtypeStruct(shape, F32)] * 2,
         scratch_shapes=[
-            pltpu.VMEM((ranks,) + x.shape, F32), dma((1,)), dma((ranks,)), dma((ranks,)),
+            pltpu.VMEM((16, TILE), F32), pltpu.VMEM((ranks, 16, TILE), F32),
+            dma((1,)), dma((ranks,)), dma((ranks,)),
         ],
         compiler_params=params(collective_id=1, has_side_effects=True),
-        name="total",
-    )(x)
+        name="solve",
+    )(*bases, polar)
+
+
+def fixed_rows(points):
+    half_size = GRID // 2
+    freq = np.arange(GRID)
+    mode_num = np.where(freq <= half_size, freq, freq - half_size)
+    angle = (mode_num[:, None] * points[None, :] % GRID) * (2.0 * np.pi / GRID)
+    return np.where((freq <= half_size)[:, None], np.cos(angle), np.sin(angle)).astype(np.float32)
 
 
 def per_device(positions, field, inv_polar, x_spline, yz_spline, tile_list, tile_count):
@@ -374,15 +445,16 @@
         return x.reshape(-1, blocks, TILE).transpose(1, 0, 2)
 
     all_freq = jnp.arange(GRID, dtype=jnp.int32)
-    fourier_rows = basis_rows(GRID, all_freq)
+    fourier_rows = jnp.asarray(fixed_rows(np.arange(GRID)))
     ky_freq = rank_index * ky_count + jnp.arange(ky_count, dtype=jnp.int32)
     full_modes, full_weights = mode_of(all_freq, GRID)
     ky_modes, ky_weights = mode_of(ky_freq, GRID)
     green = kernel_block(ky_modes, ky_weights, full_modes, full_weights, full_modes, full_weights)
-    source_rows = jnp.arange(ranks * extent, dtype=jnp.int32)
+    source_rows = np.arange(ranks * extent)
     points = (source_rows // extent * planes - 2 + source_rows % extent) % GRID
-    across = basis_rows(GRID, points)
-    back = across.T
+    across = fixed_rows(points)
+    back = jnp.asarray(np.ascontiguousarray(across.T))
+    across = jnp.asarray(across)
     slots = jnp.arange(tile_list.shape[1], dtype=jnp.int32)
     wanted = jnp.arange(blocks, dtype=jnp.int32)[:, None] + jnp.arange(reach, dtype=jnp.int32)
     live = (slots[None, :] < tile_count[:, None])[:, :, None]
@@ -395,8 +467,7 @@
     spec_shape = jax.ShapeDtypeStruct((ranks, extent, 8, GRID), F32)
     rows_shape = jax.ShapeDtypeStruct((blocks, 3, TILE), F32)
 
-    def apply(vector):
-        pv = jnp.concatenate([pos, vector, jnp.zeros((blocks, 2, TILE), F32)], axis=1)
+    def advance(pv):
         spec = pl.pallas_call(
             functools.partial(spread_kernel, planes, ky_count),
             in_specs=[VMEM] * 4,
@@ -419,47 +490,25 @@
             compiler_params=params(),
             name="pair",
         )(near, pv, before, after)
-        far = pl.pallas_call(
+        return pl.pallas_call(
             functools.partial(gather_kernel, planes, ky_count),
-            in_specs=[VMEM] * 4,
-            out_specs=VMEM,
-            out_shape=rows_shape,
+            in_specs=[VMEM] * 7,
+            out_specs=[VMEM] * 2,
+            out_shape=[rows_shape, jax.ShapeDtypeStruct((blocks, 8, TILE), F32)],
             scratch_shapes=[
                 pltpu.VMEM((extent, GRID, 2 * GRID), BF16),
                 pltpu.VMEM((extent, GRID, GRID), BF16),
             ],
             compiler_params=params(),
             name="gather",
-        )(ret, xs, yft, zft)
-        return polar * vector + far - pair
-
-    def paired(residual, precond, applied):
-        first = jnp.sum(residual * precond, axis=(0, 1))
-        second = jnp.sum(applied * precond, axis=(0, 1))
-        sums = total(jnp.stack([first, second] + [jnp.zeros_like(first)] * 6), ranks)
-        sums = jnp.sum(sums, axis=1)
-        return sums[0], sums[1]
-
-    residual = blocked(field)
-    dipoles = jnp.zeros_like(residual)
-    precond = residual / polar
-    applied = apply(precond)
-    rz_now, curvature = paired(residual, precond, applied)
-    step_size = rz_now / curvature
-    direction = precond
-    applied_dir = applied
-    for sweep_index in range(ITERS):
-        dipoles = dipoles + step_size * direction
-        residual = residual - step_size * applied_dir
-        if sweep_index + 1 < ITERS:
-            precond = residual / polar
-            applied = apply(precond)
-            rz_next, curvature = paired(residual, precond, applied)
-            beta_ratio = rz_next / rz_now
-            step_size = rz_next / (curvature - beta_ratio * rz_next / step_size)
-            direction = precond + beta_ratio * direction
-            applied_dir = applied + beta_ratio * applied_dir
-            rz_now = rz_next
+        )(ret, xs, yft, zft, pair, pv, polar)
+
+    bases = [blocked(field)]
+    pv = jnp.concatenate([pos, bases[0] / polar, jnp.zeros((blocks, 2, TILE), F32)], axis=1)
+    for sweep in range(ITERS):
+        following, pv = advance(pv)
+        bases.append(following)
+    dipoles, residual = solve(bases, polar, ranks)
 
     def flat(x):
         return x.transpose(1, 0, 2).reshape(3, atoms_here)

time: 256 us -> 215 us (0.84)
  Pallas kernels: 221 us -> 203 us
  other arithmetic: 16.8 us -> 4.07 us
  between operations: 10.9 us -> 0.71 us
    pallas_call x12 -> x10, Pallas kernels: 96.5 us -> 68.9 us  [the longest x3 22 us: advance(): pl.pallas_call(pair_kernel, in_specs=[pl.BlockSpec(memory_space=pltpu.SME...]
    pallas_call x3, Pallas kernels: 117 us -> 127 us  [middle(): pl.pallas_call(functools.partial(middle_kernel, ranks, ky_count), in_spec...]
    reduce_sum x6 -> x0, other arithmetic: 4.65 us -> none  [the longest x3 2.4 us: paired(): sums = jnp.sum(sums, axis=1)]
    select_n x5 -> x0, other arithmetic: 3.33 us -> none  [the longest x3 3.31 us: basis_rows(): jnp.where((freq <= half_size)[:, None], jnp.cos(angle), jnp.sin(angle))]
    unnamed x14 -> x4, local copies, waits for them, and re-layouts: 1.58 us -> 4.21 us
where the time goes in v1:
time: 215 us; the launch traced here: 213 us
  Pallas kernels  203 us (94%)
  local copies, waits for them, and re-layouts  5.49 us (3%)
  other arithmetic  4.07 us (2%)
    pallas_call x3, Pallas kernels, middle(): pl.pallas_call(functools.partial(middle_kernel, ranks, ky_count), in_spec...  127 us
    pallas_call x3, Pallas kernels, advance(): pl.pallas_call(pair_kernel, in_specs=[pl.BlockSpec(memory_space=pltpu.SME...  22 us
    pallas_call x3, Pallas kernels, advance(): pl.pallas_call(functools.partial(gather_kernel, planes, ky_count), in_spe...  16.2 us
    pallas_call x3, Pallas kernels, advance(): pl.pallas_call(functools.partial(spread_kernel, planes, ky_count), in_spe...  15.9 us
    pallas_call x1, Pallas kernels, solve(): pl.pallas_call(functools.partial(solve_kernel, ranks), in_specs=[VMEM] *...  14.7 us
    pallas_call x1, Pallas kernels, prepare(): pl.pallas_call(prep_kernel, grid=(blocks,), in_specs=[pl.BlockSpec((4, TI...  6.84 us

profile of v1, /device:TPU:0, one launch (start us, length us, event | category | flops | bytes accessed | tf_op | source)
XLA Modules:
  0.0 213.5 jit_solution(15927267549325412303)
XLA Ops:
  0.7 0.7 iota_compare_fusion
  1.5 0.8 copy.16
  2.3 0.6 reshape.148.near_ref
  2.9 0.7 broadcast_divide_fusion
  3.6 1.4 maximum_maximum_fusion.pv_ref
  5.0 0.8 copy.14
  5.9 0.6 copy.18
  6.5 1.1 fusion.5.green_ref
  7.6 6.8 %prep.1 = (f32[8,2,128,128]{3,2,1,0:T(8,128)}, bf16[8,256,256]{2,1,0:T(8,128)(2,1)}, bf16[8,256,256]{2,1,0:T(8,128)(2,1)}) custom-call(f32[4,1024,128]{2,1,0:T(8,128)} %yz_ref.1, f32[128,128]{1,0:T(8,128)} %constant.14.clone.rows_ref), custom_call_target="tpu_custom_call" | custom-call | tf_op jit(solution)/shard_map/prep/pallas_call | solution.py:87
  14.4 5.3 %spread.3.spec_ref = f32[16,12,8,128]{3,2,1,0:T(8,128)} custom-call(f32[8,8,128]{2,1,0:T(8,128)} %maximum_maximum_fusion.pv_ref, f32[8,10,128]{2,1,0:T(8,128)} %bitcast.18, f32[8,2,128,128]{3,2,1,0:T(8,128)} %get-tuple-element.21.yft_ref, bf16[8,256,256]{2,1,0:T(8,128)(2,1)} %get-tuple-element.22.zf_ref), custom_call_target="tpu_custom_call" | custom-call | tf_op jit(solution)/shard_map/spread/pallas_call | solution.py:471
  19.7 40.1 %middle.3 = (f32[16,12,8,128]{3,2,1,0:T(8,128)}, f32[3,8,128]{2,1,0:T(8,128)}, f32[3,8,128]{2,1,0:T(8,128)}) custom-call(f32[16,12,8,128]{3,2,1,0:T(8,128)} %spread.3.spec_ref, f32[8,8,128]{2,1,0:T(8,128)} %maximum_maximum_fusion.pv_ref, f32[8,128,128]{2,1,0:T(8,128)} %fusion.5.green_ref, f32[128,192]{1,0:T(8,128)} %constant.39.clone.across_ref, ...), custom_call_target="tpu_custom_call" | custom-call | tf_op jit(solution)/shard_map/middle/pallas_call | solution.py:331
  59.8 7.3 %pair.3.pair_ref = f32[8,3,128]{2,1,0:T(4,128)} custom-call(s32[56]{0:T(128)} %reshape.148.near_ref, f32[8,8,128]{2,1,0:T(8,128)} %maximum_maximum_fusion.pv_ref, f32[3,8,128]{2,1,0:T(8,128)} %get-tuple-element.25.before_ref, f32[3,8,128]{2,1,0:T(8,128)} %get-tuple-element.26.after_ref), custom_call_target="tpu_custom_call" | custom-call | tf_op jit(solution)/shard_map/pair/pallas_call | solution.py:480
  67.1 5.4 %gather.3 = (f32[8,3,128]{2,1,0:T(4,128)}, f32[8,8,128]{2,1,0:T(8,128)}) custom-call(f32[16,12,8,128]{3,2,1,0:T(8,128)} %get-tuple-element.23.ret_ref, f32[8,10,128]{2,1,0:T(8,128)} %bitcast.19, f32[8,2,128,128]{3,2,1,0:T(8,128)} %get-tuple-element.21.yft_ref, bf16[8,256,256]{2,1,0:T(8,128)(2,1)} %get-tuple-element.24.zft_ref, f32[8,3,128]{2,1,0:T(4,128)} %pair.3.pair_ref, ...), custom_call_target="tpu_custom_call" | custom-call | tf_op jit(solution)/shard_map/gather/pallas_call | solution.py:493
  72.5 5.3 %spread.4.spec_ref = f32[16,12,8,128]{3,2,1,0:T(8,128)} custom-call(f32[8,8,128]{2,1,0:T(8,128)} %get-tuple-element.28.pv_ref, f32[8,10,128]{2,1,0:T(8,128)} %bitcast.20, f32[8,2,128,128]{3,2,1,0:T(8,128)} %get-tuple-element.21.yft_ref, bf16[8,256,256]{2,1,0:T(8,128)(2,1)} %get-tuple-element.22.zf_ref), custom_call_target="tpu_custom_call" | custom-call | tf_op jit(solution)/shard_map/spread/pallas_call | solution.py:471
  77.8 43.7 %middle.4 = (f32[16,12,8,128]{3,2,1,0:T(8,128)}, f32[3,8,128]{2,1,0:T(8,128)}, f32[3,8,128]{2,1,0:T(8,128)}) custom-call(f32[16,12,8,128]{3,2,1,0:T(8,128)} %spread.4.spec_ref, f32[8,8,128]{2,1,0:T(8,128)} %get-tuple-element.28.pv_ref, f32[8,128,128]{2,1,0:T(8,128)} %fusion.5.green_ref, f32[128,192]{1,0:T(8,128)} %constant.39.clone.across_ref, ...), custom_call_target="tpu_custom_call" | custom-call | tf_op jit(solution)/shard_map/middle/pallas_call | solution.py:331
  121.5 7.3 %pair.4.pair_ref = f32[8,3,128]{2,1,0:T(4,128)} custom-call(s32[56]{0:T(128)} %reshape.148.near_ref, f32[8,8,128]{2,1,0:T(8,128)} %get-tuple-element.28.pv_ref, f32[3,8,128]{2,1,0:T(8,128)} %get-tuple-element.30.before_ref, f32[3,8,128]{2,1,0:T(8,128)} %get-tuple-element.31.after_ref), custom_call_target="tpu_custom_call" | custom-call | tf_op jit(solution)/shard_map/pair/pallas_call | solution.py:480
  128.9 5.4 %gather.4 = (f32[8,3,128]{2,1,0:T(4,128)}, f32[8,8,128]{2,1,0:T(8,128)}) custom-call(f32[16,12,8,128]{3,2,1,0:T(8,128)} %get-tuple-element.29.ret_ref, f32[8,10,128]{2,1,0:T(8,128)} %bitcast.21, f32[8,2,128,128]{3,2,1,0:T(8,128)} %get-tuple-element.21.yft_ref, bf16[8,256,256]{2,1,0:T(8,128)(2,1)} %get-tuple-element.24.zft_ref, f32[8,3,128]{2,1,0:T(4,128)} %pair.4.pair_ref, ...), custom_call_target="tpu_custom_call" | custom-call | tf_op jit(solution)/shard_map/gather/pallas_call | solution.py:493
  134.3 5.3 %spread.5.spec_ref = f32[16,12,8,128]{3,2,1,0:T(8,128)} custom-call(f32[8,8,128]{2,1,0:T(8,128)} %get-tuple-element.33.pv_ref, f32[8,10,128]{2,1,0:T(8,128)} %bitcast.22, f32[8,2,128,128]{3,2,1,0:T(8,128)} %get-tuple-element.21.yft_ref, bf16[8,256,256]{2,1,0:T(8,128)(2,1)} %get-tuple-element.22.zf_ref), custom_call_target="tpu_custom_call" | custom-call | tf_op jit(solution)/shard_map/spread/pallas_call | solution.py:471
  139.6 43.7 %middle.5 = (f32[16,12,8,128]{3,2,1,0:T(8,128)}, f32[3,8,128]{2,1,0:T(8,128)}, f32[3,8,128]{2,1,0:T(8,128)}) custom-call(f32[16,12,8,128]{3,2,1,0:T(8,128)} %spread.5.spec_ref, f32[8,8,128]{2,1,0:T(8,128)} %get-tuple-element.33.pv_ref, f32[8,128,128]{2,1,0:T(8,128)} %fusion.5.green_ref, f32[128,192]{1,0:T(8,128)} %constant.39.clone.across_ref, ...), custom_call_target="tpu_custom_call" | custom-call | tf_op jit(solution)/shard_map/middle/pallas_call | solution.py:331
  183.3 7.3 %pair.5.pair_ref = f32[8,3,128]{2,1,0:T(4,128)} custom-call(s32[56]{0:T(128)} %reshape.148.near_ref, f32[8,8,128]{2,1,0:T(8,128)} %get-tuple-element.33.pv_ref, f32[3,8,128]{2,1,0:T(8,128)} %get-tuple-element.35.before_ref, f32[3,8,128]{2,1,0:T(8,128)} %get-tuple-element.36.after_ref), custom_call_target="tpu_custom_call" | custom-call | tf_op jit(solution)/shard_map/pair/pallas_call | solution.py:480
  190.6 5.4 %gather.5 = (f32[8,3,128]{2,1,0:T(4,128)}, f32[8,8,128]{2,1,0:T(8,128)}) custom-call(f32[16,12,8,128]{3,2,1,0:T(8,128)} %get-tuple-element.34.ret_ref, f32[8,10,128]{2,1,0:T(8,128)} %bitcast.23, f32[8,2,128,128]{3,2,1,0:T(8,128)} %get-tuple-element.21.yft_ref, bf16[8,256,256]{2,1,0:T(8,128)(2,1)} %get-tuple-element.24.zft_ref, f32[8,3,128]{2,1,0:T(4,128)} %pair.5.pair_ref, ...), custom_call_target="tpu_custom_call" | custom-call | tf_op jit(solution)/shard_map/gather/pallas_call | solution.py:493
  196.0 14.7 %solve.1 = (f32[8,3,128]{2,1,0:T(4,128)}, f32[8,3,128]{2,1,0:T(4,128)}) custom-call(f32[8,3,128]{2,1,0:T(4,128)} %bitcast.29, f32[8,3,128]{2,1,0:T(4,128)} %get-tuple-element.27.b1_ref, f32[8,3,128]{2,1,0:T(4,128)} %get-tuple-element.32.b2_ref, f32[8,3,128]{2,1,0:T(4,128)} %get-tuple-element.37.b3_ref, f32[8,1,128]{2,1,0:T(1,128)} %bitcast.28), custom_call_target="tpu_custom_call" | custom-call | tf_op jit(solution)/shard_map/solve/pallas_call | solution.py:412
  210.8 1.3 copy.21
  212.1 1.3 copy.22
  (9 shorter events, 0.3 us)

commit v2 on v1

--- a/solution.py
+++ b/solution.py
@@ -173,56 +173,55 @@
     lax.fori_loop(0, blocks, one_block, 0)
 
 
-def pair_kernel(near_ref, pv_ref, before_ref, after_ref, out_ref, ext_ref, col_ref, acc_ref):
+def pair_sum(near_ref, pv_ref, before_ref, after_ref, out_ref, ext_ref, col_ref):
     blocks = pv_ref.shape[0]
-    ext_blocks = ext_ref.shape[0]
     reach = 2 * HALO_BLK + 1
     first_row = lax.broadcasted_iota(jnp.int32, (HALO_BLK, 8, TILE), 1) == 0
     ext_ref[:HALO_BLK] = before_ref[...] + jnp.where(first_row, -1.0 * blocks, 0.0)
     ext_ref[HALO_BLK : HALO_BLK + blocks] = pv_ref[...]
     ext_ref[HALO_BLK + blocks :] = after_ref[...] + jnp.where(first_row, 1.0 * blocks, 0.0)
-    acc_ref[...] = jnp.zeros_like(acc_ref)
     lag = lax.broadcasted_iota(jnp.int32, (8, TILE), 1) - lax.broadcasted_iota(
         jnp.int32, (8, TILE), 0
     )
 
-    def one_source(e, carry):
+    def spread_columns(e, carry):
         for c in range(6):
-            col_ref[c] = jnp.broadcast_to(ext_ref[e, c : c + 1, :], (TILE, TILE)).T
-
-        def one_home(b, inner):
-            @pl.when(near_ref[b * reach + e - b] > 0)
-            def _():
-                home = [jnp.broadcast_to(pv_ref[b, c : c + 1, :], (8, TILE)) for c in range(3)]
-                shift = jnp.where(e == b + HALO_BLK, 0, 4 * TILE)
-                direct = [jnp.zeros((8, TILE), F32) for c in range(3)]
-                tilted = [jnp.zeros((8, TILE), F32) for c in range(3)]
-                for j in range(TILE // 8):
-                    rows = slice(8 * j, 8 * j + 8)
-                    r = [home[c] - col_ref[c, rows, :] for c in range(3)]
-                    v = [col_ref[3 + c, rows, :] for c in range(3)]
-                    inverse = lax.rsqrt(r[0] * r[0] + r[1] * r[1] + r[2] * r[2] + 1.0)
-                    inverse = jnp.where(lag != 8 * j + shift, inverse, 0.0)
-                    square = inverse * inverse
-                    third = square * inverse
-                    weight = third * square * (r[0] * v[0] + r[1] * v[1] + r[2] * v[2])
-                    for c in range(3):
-                        direct[c] += third * v[c]
-                        tilted[c] += weight * r[c]
+            col_ref[e, c] = jnp.broadcast_to(ext_ref[e, c : c + 1, :], (TILE, TILE)).T
+        return carry
+
+    lax.fori_loop(0, blocks + 2 * HALO_BLK, spread_columns, 0)
+
+    def one_home(b, carry):
+        home = [jnp.broadcast_to(pv_ref[b, c : c + 1, :], (8, TILE)) for c in range(3)]
+
+        def one_source(k, sums):
+            shift = jnp.where(k == HALO_BLK, 0, 4 * TILE)
+            direct = [jnp.zeros((8, TILE), F32) for c in range(3)]
+            tilted = [jnp.zeros((8, TILE), F32) for c in range(3)]
+            for j in range(TILE // 8):
+                rows = slice(8 * j, 8 * j + 8)
+                r = [home[c] - col_ref[b + k, c, rows, :] for c in range(3)]
+                v = [col_ref[b + k, 3 + c, rows, :] for c in range(3)]
+                inverse = lax.rsqrt(r[0] * r[0] + r[1] * r[1] + r[2] * r[2] + 1.0)
+                inverse = jnp.where(lag != 8 * j + shift, inverse, 0.0)
+                square = inverse * inverse
+                third = square * inverse
+                weight = third * square * (r[0] * v[0] + r[1] * v[1] + r[2] * v[2])
                 for c in range(3):
-                    acc_ref[b, c] += direct[c] - 3.0 * tilted[c]
-
-            return inner
-
-        lo = jnp.maximum(e - (reach - 1), 0)
-        hi = jnp.minimum(e + 1, blocks)
-        lax.fori_loop(lo, hi, one_home, 0)
-        return carry
-
-    lax.fori_loop(0, ext_blocks, one_source, 0)
-    for b in range(blocks):
-        for c in range(3):
-            out_ref[b, c : c + 1] = PAIR_C * jnp.sum(acc_ref[b, c], axis=0, keepdims=True)
+                    direct[c] += third * v[c]
+                    tilted[c] += weight * r[c]
+            near = near_ref[b * reach + k]
+            return tuple(
+                sums[c] + near * (direct[c] - 3.0 * tilted[c]) for c in range(3)
+            )
+
+        sums = lax.fori_loop(0, reach, one_source, (jnp.zeros((8, TILE), F32),) * 3)
+        out_ref[b] = PAIR_C * jnp.concatenate(
+            [jnp.sum(t, axis=0, keepdims=True) for t in sums], axis=0
+        )
+        return carry
+
+    lax.fori_loop(0, blocks, one_home, 0)
 
 
 def greet(ranks, me):
@@ -273,9 +272,9 @@
 
 
 def middle_kernel(
-    ranks, ky_count, spec_ref, pv_ref, green_ref, across_ref, back_ref,
-    ret_ref, before_ref, after_ref,
-    recv_ref, done_ref, local_sems, send1, recv1, send2, recv2, halo_send, halo_recv,
+    ranks, ky_count, near_ref, spec_ref, pv_ref, green_ref, across_ref, back_ref,
+    ret_ref, pair_ref,
+    before_ref, after_ref, ext_ref, col_ref, recv_ref, done_ref, local_sems, send1, recv1, send2, recv2, halo_send, halo_recv,
 ):
     me = lax.axis_index("gx")
     blocks = pv_ref.shape[0]
@@ -322,18 +321,27 @@
     )
     for halo in halos:
         halo.wait()
+    pair_sum(near_ref, pv_ref, before_ref, after_ref, pair_ref, ext_ref, col_ref)
     wait()
 
 
-def middle(spec, pv, green, across, back, ranks, ky_count):
+def middle(near, spec, pv, green, across, back, ranks, ky_count):
     dma = pltpu.SemaphoreType.DMA
-    halo = jax.ShapeDtypeStruct((HALO_BLK, 8, TILE), F32)
+    blocks = pv.shape[0]
+    halo = pltpu.VMEM((HALO_BLK, 8, TILE), F32)
     return pl.pallas_call(
         functools.partial(middle_kernel, ranks, ky_count),
-        in_specs=[VMEM] * 5,
-        out_specs=[VMEM] * 3,
-        out_shape=[jax.ShapeDtypeStruct(spec.shape, F32), halo, halo],
+        in_specs=[pl.BlockSpec(memory_space=pltpu.SMEM)] + [VMEM] * 5,
+        out_specs=[VMEM] * 2,
+        out_shape=[
+            jax.ShapeDtypeStruct(spec.shape, F32),
+            jax.ShapeDtypeStruct((blocks, 3, TILE), F32),
+        ],
         scratch_shapes=[
+            halo,
+            halo,
+            pltpu.VMEM((blocks + 2 * HALO_BLK, 8, TILE), F32),
+            pltpu.VMEM((blocks + 2 * HALO_BLK, 6, TILE, TILE), F32),
             pltpu.VMEM(spec.shape, F32),
             pltpu.VMEM(spec.shape, F32),
             dma((2,)), dma((ranks,)), dma((ranks,)), dma((ranks,)), dma((ranks,)),
@@ -341,7 +349,7 @@
         ],
         compiler_params=params(collective_id=0, has_side_effects=True),
         name="middle",
-    )(spec, pv, green, across, back)
+    )(near, spec, pv, green, across, back)
 
 
 def combine(weights, parts):
@@ -459,7 +467,7 @@
     wanted = jnp.arange(blocks, dtype=jnp.int32)[:, None] + jnp.arange(reach, dtype=jnp.int32)
     live = (slots[None, :] < tile_count[:, None])[:, :, None]
     near = jnp.any((tile_list[:, :, None] == wanted[:, None, :]) & live, axis=1)
-    near = near.astype(jnp.int32).reshape(-1)
+    near = near.astype(F32).reshape(-1)
     yft, zf, zft = prepare(yz_spline, fourier_rows, blocks)
     xs = blocked(x_spline.reshape(2 * ORDER, atoms_here))
     pos = blocked(positions)
@@ -476,20 +484,7 @@
             compiler_params=params(),
             name="spread",
         )(pv, xs, yft, zf)
-        ret, before, after = middle(spec, pv, green, across, back, ranks, ky_count)
-        pair = pl.pallas_call(
-            pair_kernel,
-            in_specs=[pl.BlockSpec(memory_space=pltpu.SMEM)] + [VMEM] * 3,
-            out_specs=VMEM,
-            out_shape=rows_shape,
-            scratch_shapes=[
-                pltpu.VMEM((blocks + 2 * HALO_BLK, 8, TILE), F32),
-                pltpu.VMEM((6, TILE, TILE), F32),
-                pltpu.VMEM((blocks, 3, 8, TILE), F32),
-            ],
-            compiler_params=params(),
-            name="pair",
-        )(near, pv, before, after)
+        ret, pair = middle(near, spec, pv, green, across, back, ranks, ky_count)
         return pl.pallas_call(
             functools.partial(gather_kernel, planes, ky_count),
             in_specs=[VMEM] * 7,

time: 215 us -> 195 us (0.907)
  Pallas kernels: 203 us -> 183 us
    pallas_call x3 -> x0, Pallas kernels: 22 us -> none  [advance(): pl.pallas_call(pair_kernel, in_specs=[pl.BlockSpec(memory_space=pltpu.SME...]
where the time goes in v2:
time: 195 us; the launch traced here: 194 us
  Pallas kernels  183 us (94%)
  local copies, waits for them, and re-layouts  5.59 us (3%)
  other arithmetic  4.07 us (2%)
    pallas_call x3, Pallas kernels, middle(): pl.pallas_call(functools.partial(middle_kernel, ranks, ky_count), in_spec...  129 us
    pallas_call x3, Pallas kernels, advance(): pl.pallas_call(functools.partial(gather_kernel, planes, ky_count), in_spe...  16.2 us
    pallas_call x3, Pallas kernels, advance(): pl.pallas_call(functools.partial(spread_kernel, planes, ky_count), in_spe...  16 us
    pallas_call x1, Pallas kernels, solve(): pl.pallas_call(functools.partial(solve_kernel, ranks), in_specs=[VMEM] *...  15.3 us
    pallas_call x1, Pallas kernels, prepare(): pl.pallas_call(prep_kernel, grid=(blocks,), in_specs=[pl.BlockSpec((4, TI...  6.84 us
    unnamed x4, local copies, waits for them, and re-layouts  4.21 us

profile of v2, /device:TPU:0, one launch (start us, length us, event | category | flops | bytes accessed | tf_op | source)
XLA Modules:
  0.0 193.8 jit_solution(18292863747286540626)
XLA Ops:
  0.6 0.1 pad.2.clone
  0.7 0.7 iota_compare_fusion
  1.4 0.1 broadcast_add_fusion
  1.5 0.8 copy.14
  2.2 0.1 and_reduce_fusion
  2.3 0.7 reshape.148.near_ref
  3.0 0.7 broadcast_divide_fusion
  3.7 1.4 maximum_maximum_fusion.pv_ref
  5.1 0.8 copy.15
  6.0 0.6 copy.18
  6.6 1.1 fusion.5.green_ref
  7.7 6.8 %prep.1 = (f32[8,2,128,128]{3,2,1,0:T(8,128)}, bf16[8,256,256]{2,1,0:T(8,128)(2,1)}, bf16[8,256,256]{2,1,0:T(8,128)(2,1)}) custom-call(f32[4,1024,128]{2,1,0:T(8,128)} %yz_ref.1, f32[128,128]{1,0:T(8,128)} %constant.14.clone.rows_ref), custom_call_target="tpu_custom_call" | custom-call | tf_op jit(solution)/shard_map/prep/pallas_call | solution.py:87
  14.5 5.3 %spread.3.spec_ref = f32[16,12,8,128]{3,2,1,0:T(8,128)} custom-call(f32[8,8,128]{2,1,0:T(8,128)} %maximum_maximum_fusion.pv_ref, f32[8,10,128]{2,1,0:T(8,128)} %bitcast.18, f32[8,2,128,128]{3,2,1,0:T(8,128)} %get-tuple-element.18.yft_ref, bf16[8,256,256]{2,1,0:T(8,128)(2,1)} %get-tuple-element.19.zf_ref), custom_call_target="tpu_custom_call" | custom-call | tf_op jit(solution)/shard_map/spread/pallas_call | solution.py:479
  19.8 40.3 %middle.3 = (f32[16,12,8,128]{3,2,1,0:T(8,128)}, f32[8,3,128]{2,1,0:T(4,128)}) custom-call(f32[56]{0:T(128)} %reshape.148.near_ref, f32[16,12,8,128]{3,2,1,0:T(8,128)} %spread.3.spec_ref, f32[8,8,128]{2,1,0:T(8,128)} %maximum_maximum_fusion.pv_ref, f32[8,128,128]{2,1,0:T(8,128)} %fusion.5.green_ref, f32[128,192]{1,0:T(8,128)} %constant.39.clone.across_ref, ...), custom_call_target="tpu_custom_call" | custom-call | tf_op jit(solution)/shard_map/middle/pallas_call | solution.py:332
  60.1 5.4 %gather.3 = (f32[8,3,128]{2,1,0:T(4,128)}, f32[8,8,128]{2,1,0:T(8,128)}) custom-call(f32[16,12,8,128]{3,2,1,0:T(8,128)} %get-tuple-element.20.ret_ref, f32[8,10,128]{2,1,0:T(8,128)} %bitcast.19, f32[8,2,128,128]{3,2,1,0:T(8,128)} %get-tuple-element.18.yft_ref, bf16[8,256,256]{2,1,0:T(8,128)(2,1)} %get-tuple-element.21.zft_ref, ...), custom_call_target="tpu_custom_call" | custom-call | tf_op jit(solution)/shard_map/gather/pallas_call | solution.py:488
  65.5 5.3 %spread.4.spec_ref = f32[16,12,8,128]{3,2,1,0:T(8,128)} custom-call(f32[8,8,128]{2,1,0:T(8,128)} %get-tuple-element.24.pv_ref, f32[8,10,128]{2,1,0:T(8,128)} %bitcast.20, f32[8,2,128,128]{3,2,1,0:T(8,128)} %get-tuple-element.18.yft_ref, bf16[8,256,256]{2,1,0:T(8,128)(2,1)} %get-tuple-element.19.zf_ref), custom_call_target="tpu_custom_call" | custom-call | tf_op jit(solution)/shard_map/spread/pallas_call | solution.py:479
  70.9 44.5 %middle.4 = (f32[16,12,8,128]{3,2,1,0:T(8,128)}, f32[8,3,128]{2,1,0:T(4,128)}) custom-call(f32[56]{0:T(128)} %reshape.148.near_ref, f32[16,12,8,128]{3,2,1,0:T(8,128)} %spread.4.spec_ref, f32[8,8,128]{2,1,0:T(8,128)} %get-tuple-element.24.pv_ref, f32[8,128,128]{2,1,0:T(8,128)} %fusion.5.green_ref, f32[128,192]{1,0:T(8,128)} %constant.39.clone.across_ref, ...), custom_call_target="tpu_custom_call" | custom-call | tf_op jit(solution)/shard_map/middle/pallas_call | solution.py:332
  115.4 5.4 %gather.4 = (f32[8,3,128]{2,1,0:T(4,128)}, f32[8,8,128]{2,1,0:T(8,128)}) custom-call(f32[16,12,8,128]{3,2,1,0:T(8,128)} %get-tuple-element.25.ret_ref, f32[8,10,128]{2,1,0:T(8,128)} %bitcast.21, f32[8,2,128,128]{3,2,1,0:T(8,128)} %get-tuple-element.18.yft_ref, bf16[8,256,256]{2,1,0:T(8,128)(2,1)} %get-tuple-element.21.zft_ref, ...), custom_call_target="tpu_custom_call" | custom-call | tf_op jit(solution)/shard_map/gather/pallas_call | solution.py:488
  120.8 5.3 %spread.5.spec_ref = f32[16,12,8,128]{3,2,1,0:T(8,128)} custom-call(f32[8,8,128]{2,1,0:T(8,128)} %get-tuple-element.28.pv_ref, f32[8,10,128]{2,1,0:T(8,128)} %bitcast.22, f32[8,2,128,128]{3,2,1,0:T(8,128)} %get-tuple-element.18.yft_ref, bf16[8,256,256]{2,1,0:T(8,128)(2,1)} %get-tuple-element.19.zf_ref), custom_call_target="tpu_custom_call" | custom-call | tf_op jit(solution)/shard_map/spread/pallas_call | solution.py:479
  126.1 44.4 %middle.5 = (f32[16,12,8,128]{3,2,1,0:T(8,128)}, f32[8,3,128]{2,1,0:T(4,128)}) custom-call(f32[56]{0:T(128)} %reshape.148.near_ref, f32[16,12,8,128]{3,2,1,0:T(8,128)} %spread.5.spec_ref, f32[8,8,128]{2,1,0:T(8,128)} %get-tuple-element.28.pv_ref, f32[8,128,128]{2,1,0:T(8,128)} %fusion.5.green_ref, f32[128,192]{1,0:T(8,128)} %constant.39.clone.across_ref, ...), custom_call_target="tpu_custom_call" | custom-call | tf_op jit(solution)/shard_map/middle/pallas_call | solution.py:332
  170.5 5.4 %gather.5 = (f32[8,3,128]{2,1,0:T(4,128)}, f32[8,8,128]{2,1,0:T(8,128)}) custom-call(f32[16,12,8,128]{3,2,1,0:T(8,128)} %get-tuple-element.29.ret_ref, f32[8,10,128]{2,1,0:T(8,128)} %bitcast.23, f32[8,2,128,128]{3,2,1,0:T(8,128)} %get-tuple-element.18.yft_ref, bf16[8,256,256]{2,1,0:T(8,128)(2,1)} %get-tuple-element.21.zft_ref, ...), custom_call_target="tpu_custom_call" | custom-call | tf_op jit(solution)/shard_map/gather/pallas_call | solution.py:488
  175.9 15.3 %solve.1 = (f32[8,3,128]{2,1,0:T(4,128)}, f32[8,3,128]{2,1,0:T(4,128)}) custom-call(f32[8,3,128]{2,1,0:T(4,128)} %bitcast.29, f32[8,3,128]{2,1,0:T(4,128)} %get-tuple-element.23.b1_ref, f32[8,3,128]{2,1,0:T(4,128)} %get-tuple-element.27.b2_ref, f32[8,3,128]{2,1,0:T(4,128)} %get-tuple-element.31.b3_ref, f32[8,1,128]{2,1,0:T(1,128)} %bitcast.28), custom_call_target="tpu_custom_call" | custom-call | tf_op jit(solution)/shard_map/solve/pallas_call | solution.py:420
  191.2 1.3 copy.21
  192.5 1.3 copy.22
  (6 shorter events, 0.0 us)
